TPU v7x, 256 devices: a whole 4x4x8 slice. The times are simulated.
256 devices in a mesh: blk: 128 (over z, y_lo, x, core), dp: 2 (over y_hi).
Axes of the slice: x: 4, y: 4 (y_hi: 2, y_lo: 2; y = y_hi * 2 + y_lo), z: 8, core: 2. Of those that a mesh axis runs over, the one named last changes fastest.
Arguments:
- tokens: bfloat16 [49152, 2048], P(('blk', 'dp')), may hold values from -6 to 6
- cotangent: bfloat16 [49152, 2048], P(('blk', 'dp')), may hold values from -0.59765625 to 0.59765625
- gate_probs: bfloat16 [49152, 3], P(('blk', 'dp')), may hold values from 0.099609375 to 1
- slot_rows: int32 [384, 128], P('blk'), may hold values from 0 to 384, as said below
- w_gate: bfloat16 [128, 2048, 768], P('blk', None, 'dp'), may hold values from -0.125 to 0.125
- w_up: bfloat16 [128, 2048, 768], P('blk', None, 'dp'), may hold values from -0.125 to 0.125
- w_down: bfloat16 [128, 768, 2048], P('blk', 'dp'), may hold values from -0.21875 to 0.21875
Outputs:
- mixed: bfloat16 [49152, 2048], P(('blk', 'dp'))
- input_grad: bfloat16 [49152, 2048], P(('blk', 'dp'))
- gate_grad: float32 [49152, 3], P(('blk', 'dp'))
- w_gate_grad: bfloat16 [128, 2048, 768], P('blk', None, 'dp')
- w_up_grad: bfloat16 [128, 2048, 768], P('blk', None, 'dp')
- w_down_grad: bfloat16 [128, 768, 2048], P('blk', 'dp')
Inputs may be any that keep to these rules, and one draw needn't show every extreme that they name: `slot_rows`: entries below 384 in a row are distinct and stand before the entries equal to 384; every row names at least 16 tokens, and some row names 128.
All inputs are finite; a program needn't handle non-finite values.
Results may differ from a plain program's by a relative error of at most 0.0075.
Values may be sent and summed in bfloat16 or wider, within the bound.
A program may use at most 128 MiB of HBM per device.

v0:
```python
import jax
import jax.numpy as jnp
from jax import lax
from jax.sharding import PartitionSpec as P

BF = jnp.bfloat16
F32 = jnp.float32


def shifted(value, axis, steps):
    count = lax.axis_size(axis)
    pairs = [(source, (source + steps) % count) for source in range(count)]
    return lax.ppermute(value, axis, pairs)


def on_device(tokens, cotangent, gate_probs, slot_rows, w_gate, w_up, w_down):
    half = lax.axis_index("dp")
    own = tokens.shape[0]
    group_x = lax.all_gather(tokens, "dp", axis=0, tiled=True)
    group_dy = lax.all_gather(cotangent, "dp", axis=0, tiled=True)
    group_gate = lax.all_gather(gate_probs, "dp", axis=0, tiled=True)
    cycle, cap = slot_rows.shape
    group = group_x.shape[0]
    names = slot_rows[:, :, None] == lax.broadcasted_iota(jnp.int32, (1, 1, group), 2)
    picks = names.astype(BF)
    rows_x = jnp.einsum("sct,td->scd", picks, group_x, preferred_element_type=F32).astype(BF)
    rows_dy = jnp.einsum("sct,td->scd", picks, group_dy, preferred_element_type=F32).astype(BF)
    rows_gate = jnp.einsum("sct,ts->sc", picks, group_gate, preferred_element_type=F32).astype(BF)
    lists_x, lists_dy, lists_gate = ([rows_x[0]], [rows_dy[0]], [rows_gate[0]])
    for step in range(1, cycle):
        lists_x.append(shifted(rows_x[step], "blk", -step))
        lists_dy.append(shifted(rows_dy[step], "blk", -step))
        lists_gate.append(shifted(rows_gate[step], "blk", -step))
    x = jnp.concatenate(lists_x, axis=0)
    dy = jnp.concatenate(lists_dy, axis=0)
    gate = jnp.concatenate(lists_gate, axis=0).astype(F32)[:, None]
    w_g, w_u, w_d = (w_gate[0], w_up[0], w_down[0])
    pre_gate = jnp.dot(x, w_g, preferred_element_type=F32)
    pre_up = jnp.dot(x, w_u, preferred_element_type=F32)
    back = jnp.einsum("cd,hd->ch", dy, w_d, preferred_element_type=F32)
    sig = jax.nn.sigmoid(pre_gate)
    active = pre_gate * sig
    hidden = active * pre_up
    gate_part = jnp.sum(hidden * back, axis=1)
    hidden_w = (hidden * gate).astype(BF)
    hidden_grad = back * gate
    pgg = (hidden_grad * pre_up * sig * (1.0 + pre_gate * (1.0 - sig))).astype(BF)
    pug = (hidden_grad * active).astype(BF)
    weighted = jnp.dot(hidden_w, w_d, preferred_element_type=F32).astype(BF)
    in_grad = jnp.einsum("ch,dh->cd", pgg, w_g, preferred_element_type=F32)
    in_grad = in_grad + jnp.einsum("ch,dh->cd", pug, w_u, preferred_element_type=F32)
    in_grad = in_grad.astype(BF)
    out_w, out_i, out_g = ([weighted[:cap]], [in_grad[:cap]], [gate_part[:cap]])
    for step in range(1, cycle):
        rows = slice(step * cap, (step + 1) * cap)
        out_w.append(shifted(weighted[rows], "blk", step))
        out_i.append(shifted(in_grad[rows], "blk", step))
        out_g.append(shifted(gate_part[rows], "blk", step))
    d_gate = jnp.einsum("cd,ch->dh", x, pgg, preferred_element_type=F32).astype(BF)
    d_up = jnp.einsum("cd,ch->dh", x, pug, preferred_element_type=F32).astype(BF)
    d_down = jnp.einsum("ch,cd->hd", hidden_w, dy, preferred_element_type=F32).astype(BF)
    back_w = jnp.concatenate(out_w, axis=0)
    back_i = jnp.concatenate(out_i, axis=0)
    flat = picks.reshape(cycle * cap, group)
    mixed = jnp.einsum("ct,cd->td", flat, back_w, preferred_element_type=F32)
    input_grad = jnp.einsum("ct,cd->td", flat, back_i, preferred_element_type=F32)
    gate_grad = jnp.stack(
        [jnp.sum(jnp.where(names[s], out_g[s][:, None], 0.0), axis=0) for s in range(cycle)], axis=1
    )

    def summed(full, kind):
        mine = lax.dynamic_slice_in_dim(full, half * own, own, 0)
        other = lax.dynamic_slice_in_dim(full, (1 - half) * own, own, 0)
        arrived = lax.ppermute(other.astype(kind), "dp", [(0, 1), (1, 0)])
        return mine + arrived.astype(F32)

    return (
        summed(mixed, BF).astype(BF),
        summed(input_grad, BF).astype(BF),
        summed(gate_grad, F32),
        d_gate[None],
        d_up[None],
        d_down[None],
    )


def solution(mesh):
    in_specs = (
        P(("blk", "dp"), None),
        P(("blk", "dp"), None),
        P(("blk", "dp"), None),
        P("blk", None),
        P("blk", None, "dp"),
        P("blk", None, "dp"),
        P("blk", "dp", None),
    )
    out_specs = (
        P(("blk", "dp"), None),
        P(("blk", "dp"), None),
        P(("blk", "dp"), None),
        P("blk", None, "dp"),
        P("blk", None, "dp"),
        P("blk", "dp", None),
    )
    return jax.shard_map(
        on_device, mesh=mesh, in_specs=in_specs, out_specs=out_specs, check_vma=False
    )
```

profile of v0, /device:TPU:1, one launch (start us, length us, event | category | flops | bytes accessed | tf_op | source)
XLA Modules:
  0.0 200.9 jit_solution(9624781532558431168)
XLA Ops:
  7.2 0.7 all-gather.4.cloned.1.call-update
  8.0 0.7 all-gather.6.cloned.1.call-update
  8.7 5.5 %all-gather = bf16[2,192,3]{1,2,0:T(4,128)(2,1)S(1)} all-gather(bf16[1,192,3]{1,2,0:T(4,128)(2,1)S(1)} %bitcast.76), channel_id=1, replica_groups=mesh['blk'=128,'dp'=2] {'dp'}, dimensions={0}, use_global_device_ids=true | all-gather | bytes 3456 | tf_op jit(solution)/shard_map/all_gather | solution.py:21
  14.3 0.3 fusion.28
  14.6 8.9 %collective-permute-start.3 = (bf16[128]{0:T(256)(128)(2,1)S(1)}, bf16[128]{0:T(256)(128)(2,1)S(1)}, u32[]{:S(2)}, u32[]{:S(2)}) collective-permute-start(bf16[128]{0:T(256)(128)(2,1)S(1)} %get-tuple-element.29), channel_id=1, source_target_pairs={{0,252},{2,254},{4,0},{6,2},{8,4},{10,6},{12,8},{14,10},{16,12},{1... | collective-permute-start | bytes 776 | tf_op jit(solution)/shard_map/ppermute | solution.py:13
  23.5 2.1 %collective-permute-start.2 = (bf16[128]{0:T(256)(128)(2,1)S(1)}, bf16[128]{0:T(256)(128)(2,1)S(1)}, u32[]{:S(2)}, u32[]{:S(2)}) collective-permute-start(bf16[128]{0:T(256)(128)(2,1)S(1)} %get-tuple-element.30), channel_id=1, source_target_pairs={{0,254},{2,0},{4,2},{6,4},{8,6},{10,8},{12,10},{14,12},{16,14},{18... | collective-permute-start | bytes 776 | tf_op jit(solution)/shard_map/ppermute | solution.py:13
  25.6 0.1 iota_compare_fusion
  25.8 0.7 collective-permute-done.2
  26.5 20.7 %all-gather.4.cloned.1.call-done = bf16[384,2048]{1,0:T(8,128)(2,1)} async-done(((bf16[192,2048]{1,0:T(8,128)(2,1)}), bf16[384,2048]{1,0:T(8,128)(2,1)}) %all-gather.4.cloned.1.call-update) | async-done | bytes 1572880 | tf_op jit(solution)/shard_map/all_gather | solution.py:19
  47.3 2.4 %convolution_convert_fusion.5 = bf16[3,128,2048]{2,1,0:T(8,128)(2,1)S(1)} fusion(bf16[384,2048]{1,0:T(8,128)(2,1)} %all-gather.4.cloned.1.call-done, s32[3,128]{1,0:T(4,128)S(1)} %copy-done.3), kind=kOutput, calls=%fused_computation.6 | convolution fusion | flops 604913664 | bytes 3147264 | tf_op jit(solution)/shard_map/sct,td->scd/dot_general | solution.py:26
  49.7 0.2 slice_bitcast_fusion.5
  49.9 5.3 %collective-permute-start.1 = (bf16[128,2048]{1,0:T(8,128)(2,1)S(1)}, bf16[128,2048]{1,0:T(8,128)(2,1)}, u32[]{:S(2)}, u32[]{:S(2)}) collective-permute-start(bf16[128,2048]{1,0:T(8,128)(2,1)S(1)} %get-tuple-element.21), channel_id=1, source_target_pairs={{0,252},{2,254},{4,0},{6,2},{8,4},{10,6},{12,8},{14,10},{16,12},{1... | collective-permute-start | bytes 1572872 | tf_op jit(solution)/shard_map/ppermute | solution.py:13
  55.1 1.1 collective-permute-start
  56.3 26.1 %all-gather.6.cloned.1.call-done = bf16[384,2048]{1,0:T(8,128)(2,1)} async-done(((bf16[192,2048]{1,0:T(8,128)(2,1)}), bf16[384,2048]{1,0:T(8,128)(2,1)}) %all-gather.6.cloned.1.call-update) | async-done | bytes 1572880 | tf_op jit(solution)/shard_map/all_gather | solution.py:20
  82.3 2.4 %convolution_convert_fusion.3 = bf16[3,128,2048]{2,1,0:T(8,128)(2,1)S(1)} fusion(bf16[384,2048]{1,0:T(8,128)(2,1)} %all-gather.6.cloned.1.call-done, s32[3,128]{1,0:T(4,128)S(1)} %copy-done.3), kind=kOutput, calls=%fused_computation.4 | convolution fusion | flops 604913664 | bytes 3147264 | tf_op jit(solution)/shard_map/sct,td->scd/dot_general | solution.py:27
  84.9 10.9 %collective-permute-start.8 = (bf16[128,2048]{1,0:T(8,128)(2,1)S(1)}, bf16[128,2048]{1,0:T(8,128)(2,1)S(1)}, u32[]{:S(2)}, u32[]{:S(2)}) collective-permute-start(bf16[128,2048]{1,0:T(8,128)(2,1)S(1)} %get-tuple-element.15), channel_id=1, source_target_pairs={{0,252},{2,254},{4,0},{6,2},{8,4},{10,6},{12,8},{14,10},{16,12},{1... | collective-permute-start | bytes 1572872 | tf_op jit(solution)/shard_map/ppermute | solution.py:13
  95.8 0.8 collective-permute-start.7
  96.6 2.4 %fusion.20 = f32[384,384]{0,1:T(8,128)S(1)} fusion(bf16[1,2048,384]{2,1,0:T(8,128)(2,1)S(1)} %copy-done.2, bf16[128,2048]{1,0:T(8,128)(2,1)} %collective-permute-done.1, bf16[128,2048]{1,0:T(8,128)(2,1)} %collective-permute-done, bf16[128,2048]{1,0:T(8,128)(2,1)S(1)} %get-tuple-element.20), kind=kOutput, calls=%fused_computation.29 | convolution fusion | flops 608698368 | bytes 3735552 | tf_op jit(solution)/shard_map/dot_general | solution.py:39
  98.9 2.2 %fusion.24 = f32[384,384]{0,1:T(8,128)S(1)} fusion(bf16[1,2048,384]{2,1,0:T(8,128)(2,1)S(1)} %copy-done.1, bf16[128,2048]{1,0:T(8,128)(2,1)} %collective-permute-done.1, bf16[128,2048]{1,0:T(8,128)(2,1)} %collective-permute-done, bf16[128,2048]{1,0:T(8,128)(2,1)S(1)} %get-tuple-element.20), kind=kOutput, calls=%fused_computation.33 | convolution fusion | flops 608698368 | bytes 3735552 | tf_op jit(solution)/shard_map/dot_general | solution.py:38
  101.2 5.3 %collective-permute-done.8 = bf16[128,2048]{1,0:T(8,128)(2,1)S(1)} collective-permute-done((bf16[128,2048]{1,0:T(8,128)(2,1)S(1)}, bf16[128,2048]{1,0:T(8,128)(2,1)S(1)}, u32[]{:S(2)}, u32[]{:S(2)}) %collective-permute-start.8) | collective-permute-done | bytes 524320 | tf_op jit(solution)/shard_map/ppermute | solution.py:13
  106.5 1.2 multiply_reduce_fusion
  107.8 1.0 convolution_convert_fusion.4
  108.8 0.1 fusion.39
  109.0 2.5 %collective-permute-start.4 = (bf16[128,2048]{1,0:T(8,128)(2,1)S(1)}, bf16[128,2048]{1,0:T(8,128)(2,1)S(1)}, u32[]{:S(2)}, u32[]{:S(2)}) collective-permute-start(bf16[128,2048]{1,0:T(8,128)(2,1)S(1)} %get-tuple-element.19), channel_id=1, source_target_pairs={{0,2},{2,4},{4,6},{6,8},{8,10},{10,12},{12,14},{14,16},{16,18},{18... | collective-permute-start | bytes 1572872 | tf_op jit(solution)/shard_map/ppermute | solution.py:13
  111.5 1.0 fusion.22
  112.5 1.0 add_convert_fusion
  113.6 0.2 fusion.38
  113.7 5.0 %collective-permute-start.10 = (bf16[128,2048]{1,0:T(8,128)(2,1)S(1)}, bf16[128,2048]{1,0:T(8,128)(2,1)S(1)}, u32[]{:S(2)}, u32[]{:S(2)}) collective-permute-start(bf16[128,2048]{1,0:T(8,128)(2,1)S(1)} %get-tuple-element.12), channel_id=1, source_target_pairs={{0,4},{2,6},{4,8},{6,10},{8,12},{10,14},{12,16},{14,18},{16,20},{1... | collective-permute-start | bytes 1572872 | tf_op jit(solution)/shard_map/ppermute | solution.py:13
  118.7 3.6 %collective-permute-start.13 = (f32[128]{0:T(128)S(1)}, f32[128]{0:T(128)S(1)}, u32[]{:S(2)}, u32[]{:S(2)}) collective-permute-start(f32[128]{0:T(128)S(1)} %get-tuple-element.26), channel_id=1, source_target_pairs={{0,4},{2,6},{4,8},{6,10},{8,12},{10,14},{12,16},{14,18},{16,20},{1... | collective-permute-start | bytes 1544 | tf_op jit(solution)/shard_map/ppermute | solution.py:13
  122.3 1.1 collective-permute-start.12
  123.4 3.5 %fusion = bf16[1,2048,384]{2,1,0:T(8,128)(2,1)} fusion(bf16[384,384]{0,1:T(8,128)(2,1)S(1)} %get-tuple-element.10, bf16[128,2048]{1,0:T(8,128)(2,1)} %collective-permute-done.1, bf16[128,2048]{1,0:T(8,128)(2,1)} %collective-permute-done, bf16[128,2048]{1,0:T(8,128)(2,1)S(1)} %get-tuple-element.20), kind=kOutput, calls=%fused_computation.7 | convolution fusion | flops 609484800 | bytes 3440640 | tf_op jit(solution)/shard_map/cd,ch->dh/dot_general | solution.py:59
  126.9 3.5 %fusion.1 = bf16[1,2048,384]{2,1,0:T(8,128)(2,1)} fusion(bf16[384,384]{0,1:T(8,128)(2,1)S(1)} %get-tuple-element.24, bf16[128,2048]{1,0:T(8,128)(2,1)} %collective-permute-done.1, bf16[128,2048]{1,0:T(8,128)(2,1)} %collective-permute-done, bf16[128,2048]{1,0:T(8,128)(2,1)S(1)} %get-tuple-element.20), kind=kOutput, calls=%fused_computation.8 | convolution fusion | flops 609484800 | bytes 3440640 | tf_op jit(solution)/shard_map/cd,ch->dh/dot_general | solution.py:60
  130.5 20.4 %collective-permute-done.13 = f32[128]{0:T(128)S(1)} collective-permute-done((f32[128]{0:T(128)S(1)}, f32[128]{0:T(128)S(1)}, u32[]{:S(2)}, u32[]{:S(2)}) %collective-permute-start.13) | collective-permute-done | bytes 544 | tf_op jit(solution)/shard_map/ppermute | solution.py:13
  150.8 0.2 select_reduce_fusion.2
  151.1 4.0 %collective-permute-start.14 = (f32[192,3]{0,1:T(4,128)S(1)}, f32[192,3]{0,1:T(4,128)S(1)}, u32[]{:S(2)}, u32[]{:S(2)}) collective-permute-start(f32[192,3]{0,1:T(4,128)S(1)} %constant_dynamic-slice_fusion), channel_id=1, source_target_pairs={{0,1},{1,0},{2,3},{3,2},{4,5},{5,4},{6,7},{7,6},{8,9},{9,8},{10,11... | collective-permute-start | bytes 6920 | tf_op jit(solution)/shard_map/ppermute | solution.py:74
  155.1 1.1 fusion.3
  156.2 0.1 dynamic-slice_convert_fusion.1
  156.4 0.1 collective-permute-start.6
  156.5 0.5 collective-permute-done.9
  156.9 1.1 fusion.9
  158.0 0.1 dynamic-slice_convert_fusion
  158.2 4.1 %collective-permute-start.11 = (bf16[192,2048]{1,0:T(8,128)(2,1)S(1)}, bf16[192,2048]{1,0:T(8,128)(2,1)S(1)}, u32[]{:S(2)}, u32[]{:S(2)}) collective-permute-start(bf16[192,2048]{1,0:T(8,128)(2,1)S(1)} %dynamic-slice_convert_fusion), channel_id=1, source_target_pairs={{0,1},{1,0},{2,3},{3,2},{4,5},{5,4},{6,7},{7,6},{8,9},{9,8},{10,11... | collective-permute-start | bytes 2359304 | tf_op jit(solution)/shard_map/ppermute | solution.py:74
  162.2 2.1 %fusion.2 = bf16[1,384,2048]{2,1,0:T(8,128)(2,1)} fusion(bf16[384,384]{0,1:T(8,128)(2,1)S(1)} %get-tuple-element.23, bf16[128,2048]{1,0:T(8,128)(2,1)S(1)} %collective-permute-done.8, bf16[128,2048]{1,0:T(8,128)(2,1)S(1)} %collective-permute-done.7, bf16[128,2048]{1,0:T(8,128)(2,1)S(1)} %get-tuple-element.14), kind=kOutput, calls=%fused_computation.9 | convolution fusion | flops 609484800 | bytes 3440640 | tf_op jit(solution)/shard_map/ch,cd->hd/dot_general | solution.py:61
  164.4 0.7 dynamic-slice_add_fusion
  165.0 11.1 %collective-permute-done.6 = bf16[192,2048]{1,0:T(8,128)(2,1)S(1)} collective-permute-done((bf16[192,2048]{1,0:T(8,128)(2,1)S(1)}, bf16[192,2048]{1,0:T(8,128)(2,1)S(1)}, u32[]{:S(2)}, u32[]{:S(2)}) %collective-permute-start.6) | collective-permute-done | bytes 786464 | tf_op jit(solution)/shard_map/ppermute | solution.py:74
  176.2 1.1 add_convert_fusion.2
  177.2 15.8 %collective-permute-done.11 = bf16[192,2048]{1,0:T(8,128)(2,1)S(1)} collective-permute-done((bf16[192,2048]{1,0:T(8,128)(2,1)S(1)}, bf16[192,2048]{1,0:T(8,128)(2,1)S(1)}, u32[]{:S(2)}, u32[]{:S(2)}) %collective-permute-start.11) | collective-permute-done | bytes 786464 | tf_op jit(solution)/shard_map/ppermute | solution.py:74
  193.0 1.1 add_convert_fusion.1
  (35 shorter events, 0.6 us)
Async XLA Ops:
  7.2 99.4 %copy-start = (bf16[1,384,2048]{2,1,0:T(8,128)(2,1)S(1)}, bf16[1,384,2048]{2,1,0:T(8,128)(2,1)}, u32[]{:S(2)}) copy-start(bf16[1,384,2048]{2,1,0:T(8,128)(2,1)} %param.13) | copy-start | bytes 4718596
  7.2 1.5 copy-start.4
  7.2 7.1 %copy-start.3 = (s32[3,128]{1,0:T(4,128)S(1)}, s32[3,128]{1,0:T(4,128)}, u32[]{:S(2)}) copy-start(s32[3,128]{1,0:T(4,128)} %param.10) | copy-start | bytes 4612
  7.2 40.1 %all-gather.4.cloned.1.call-start = ((), (), s32[]{:S(2)}) async-start(), calls=%async_computation | async-start | bytes 2359296 | tf_op jit(solution)/shard_map/all_gather | solution.py:19
  7.9 74.4 %all-gather.6.cloned.1.call-start = ((), (), s32[]{:S(2)}) async-start(), calls=%async_computation.1 | async-start | bytes 2359296 | tf_op jit(solution)/shard_map/all_gather | solution.py:20
  14.6 11.2 %collective-permute-start.3 = (bf16[128]{0:T(256)(128)(2,1)S(1)}, bf16[128]{0:T(256)(128)(2,1)S(1)}, u32[]{:S(2)}, u32[]{:S(2)}) collective-permute-start(bf16[128]{0:T(256)(128)(2,1)S(1)} %get-tuple-element.29), channel_id=1, source_target_pairs={{0,252},{2,254},{4,0},{6,2},{8,4},{10,6},{12,8},{14,10},{16,12},{1... | collective-permute-start | bytes 776 | tf_op jit(solution)/shard_map/ppermute | solution.py:13
  23.5 3.0 %collective-permute-start.2 = (bf16[128]{0:T(256)(128)(2,1)S(1)}, bf16[128]{0:T(256)(128)(2,1)S(1)}, u32[]{:S(2)}, u32[]{:S(2)}) collective-permute-start(bf16[128]{0:T(256)(128)(2,1)S(1)} %get-tuple-element.30), channel_id=1, source_target_pairs={{0,254},{2,0},{4,2},{6,4},{8,6},{10,8},{12,10},{14,12},{16,14},{18... | collective-permute-start | bytes 776 | tf_op jit(solution)/shard_map/ppermute | solution.py:13
  49.9 46.7 %collective-permute-start.1 = (bf16[128,2048]{1,0:T(8,128)(2,1)S(1)}, bf16[128,2048]{1,0:T(8,128)(2,1)}, u32[]{:S(2)}, u32[]{:S(2)}) collective-permute-start(bf16[128,2048]{1,0:T(8,128)(2,1)S(1)} %get-tuple-element.21), channel_id=1, source_target_pairs={{0,252},{2,254},{4,0},{6,2},{8,4},{10,6},{12,8},{14,10},{16,12},{1... | collective-permute-start | bytes 1572872 | tf_op jit(solution)/shard_map/ppermute | solution.py:13
  55.1 41.4 %collective-permute-start = (bf16[128,2048]{1,0:T(8,128)(2,1)S(1)}, bf16[128,2048]{1,0:T(8,128)(2,1)}, u32[]{:S(2)}, u32[]{:S(2)}) collective-permute-start(bf16[128,2048]{1,0:T(8,128)(2,1)S(1)} %get-tuple-element.22), channel_id=1, source_target_pairs={{0,254},{2,0},{4,2},{6,4},{8,6},{10,8},{12,10},{14,12},{16,14},{18... | collective-permute-start | bytes 1572872 | tf_op jit(solution)/shard_map/ppermute | solution.py:13
  84.8 11.8 %copy-start.2 = (bf16[1,2048,384]{2,1,0:T(8,128)(2,1)S(1)}, bf16[1,2048,384]{2,1,0:T(8,128)(2,1)}, u32[]{:S(2)}) copy-start(bf16[1,2048,384]{2,1,0:T(8,128)(2,1)} %param.12) | copy-start | bytes 4718596
  84.9 21.7 %collective-permute-start.8 = (bf16[128,2048]{1,0:T(8,128)(2,1)S(1)}, bf16[128,2048]{1,0:T(8,128)(2,1)S(1)}, u32[]{:S(2)}, u32[]{:S(2)}) collective-permute-start(bf16[128,2048]{1,0:T(8,128)(2,1)S(1)} %get-tuple-element.15), channel_id=1, source_target_pairs={{0,252},{2,254},{4,0},{6,2},{8,4},{10,6},{12,8},{14,10},{16,12},{1... | collective-permute-start | bytes 1572872 | tf_op jit(solution)/shard_map/ppermute | solution.py:13
  95.8 10.8 %collective-permute-start.7 = (bf16[128,2048]{1,0:T(8,128)(2,1)S(1)}, bf16[128,2048]{1,0:T(8,128)(2,1)S(1)}, u32[]{:S(2)}, u32[]{:S(2)}) collective-permute-start(bf16[128,2048]{1,0:T(8,128)(2,1)S(1)} %get-tuple-element.16), channel_id=1, source_target_pairs={{0,254},{2,0},{4,2},{6,4},{8,6},{10,8},{12,10},{14,12},{16,14},{18... | collective-permute-start | bytes 1572872 | tf_op jit(solution)/shard_map/ppermute | solution.py:13
  96.6 2.4 %copy-start.1 = (bf16[1,2048,384]{2,1,0:T(8,128)(2,1)S(1)}, bf16[1,2048,384]{2,1,0:T(8,128)(2,1)}, u32[]{:S(2)}) copy-start(bf16[1,2048,384]{2,1,0:T(8,128)(2,1)} %param.11) | copy-start | bytes 4718596
  108.9 46.2 %collective-permute-start.5 = (bf16[128,2048]{1,0:T(8,128)(2,1)S(1)}, bf16[128,2048]{1,0:T(8,128)(2,1)S(1)}, u32[]{:S(2)}, u32[]{:S(2)}) collective-permute-start(bf16[128,2048]{1,0:T(8,128)(2,1)S(1)} %get-tuple-element.18), channel_id=1, source_target_pairs={{0,4},{2,6},{4,8},{6,10},{8,12},{10,14},{12,16},{14,18},{16,20},{1... | collective-permute-start | bytes 1572872 | tf_op jit(solution)/shard_map/ppermute | solution.py:13
  109.0 46.1 %collective-permute-start.4 = (bf16[128,2048]{1,0:T(8,128)(2,1)S(1)}, bf16[128,2048]{1,0:T(8,128)(2,1)S(1)}, u32[]{:S(2)}, u32[]{:S(2)}) collective-permute-start(bf16[128,2048]{1,0:T(8,128)(2,1)S(1)} %get-tuple-element.19), channel_id=1, source_target_pairs={{0,2},{2,4},{4,6},{6,8},{8,10},{10,12},{12,14},{14,16},{16,18},{18... | collective-permute-start | bytes 1572872 | tf_op jit(solution)/shard_map/ppermute | solution.py:13
  113.7 42.7 %collective-permute-start.10 = (bf16[128,2048]{1,0:T(8,128)(2,1)S(1)}, bf16[128,2048]{1,0:T(8,128)(2,1)S(1)}, u32[]{:S(2)}, u32[]{:S(2)}) collective-permute-start(bf16[128,2048]{1,0:T(8,128)(2,1)S(1)} %get-tuple-element.12), channel_id=1, source_target_pairs={{0,4},{2,6},{4,8},{6,10},{8,12},{10,14},{12,16},{14,18},{16,20},{1... | collective-permute-start | bytes 1572872 | tf_op jit(solution)/shard_map/ppermute | solution.py:13
  118.7 32.1 %collective-permute-start.13 = (f32[128]{0:T(128)S(1)}, f32[128]{0:T(128)S(1)}, u32[]{:S(2)}, u32[]{:S(2)}) collective-permute-start(f32[128]{0:T(128)S(1)} %get-tuple-element.26), channel_id=1, source_target_pairs={{0,4},{2,6},{4,8},{6,10},{8,12},{10,14},{12,16},{14,18},{16,20},{1... | collective-permute-start | bytes 1544 | tf_op jit(solution)/shard_map/ppermute | solution.py:13
  122.3 28.5 %collective-permute-start.12 = (f32[128]{0:T(128)S(1)}, f32[128]{0:T(128)S(1)}, u32[]{:S(2)}, u32[]{:S(2)}) collective-permute-start(f32[128]{0:T(128)S(1)} %get-tuple-element.25), channel_id=1, source_target_pairs={{0,2},{2,4},{4,6},{6,8},{8,10},{10,12},{12,14},{14,16},{16,18},{18... | collective-permute-start | bytes 1544 | tf_op jit(solution)/shard_map/ppermute | solution.py:13
  150.8 6.1 %collective-permute-start.9 = (bf16[128,2048]{1,0:T(8,128)(2,1)S(1)}, bf16[128,2048]{1,0:T(8,128)(2,1)S(1)}, u32[]{:S(2)}, u32[]{:S(2)}) collective-permute-start(bf16[128,2048]{1,0:T(8,128)(2,1)S(1)} %get-tuple-element.13), channel_id=1, source_target_pairs={{0,2},{2,4},{4,6},{6,8},{8,10},{10,12},{12,14},{14,16},{16,18},{18... | collective-permute-start | bytes 1572872 | tf_op jit(solution)/shard_map/ppermute | solution.py:13
  151.1 13.3 %collective-permute-start.14 = (f32[192,3]{0,1:T(4,128)S(1)}, f32[192,3]{0,1:T(4,128)S(1)}, u32[]{:S(2)}, u32[]{:S(2)}) collective-permute-start(f32[192,3]{0,1:T(4,128)S(1)} %constant_dynamic-slice_fusion), channel_id=1, source_target_pairs={{0,1},{1,0},{2,3},{3,2},{4,5},{5,4},{6,7},{7,6},{8,9},{9,8},{10,11... | collective-permute-start | bytes 6920 | tf_op jit(solution)/shard_map/ppermute | solution.py:74
  156.4 19.8 %collective-permute-start.6 = (bf16[192,2048]{1,0:T(8,128)(2,1)S(1)}, bf16[192,2048]{1,0:T(8,128)(2,1)S(1)}, u32[]{:S(2)}, u32[]{:S(2)}) collective-permute-start(bf16[192,2048]{1,0:T(8,128)(2,1)S(1)} %dynamic-slice_convert_fusion.1), channel_id=1, source_target_pairs={{0,1},{1,0},{2,3},{3,2},{4,5},{5,4},{6,7},{7,6},{8,9},{9,8},{10,11... | collective-permute-start | bytes 2359304 | tf_op jit(solution)/shard_map/ppermute | solution.py:74
  158.2 34.9 %collective-permute-start.11 = (bf16[192,2048]{1,0:T(8,128)(2,1)S(1)}, bf16[192,2048]{1,0:T(8,128)(2,1)S(1)}, u32[]{:S(2)}, u32[]{:S(2)}) collective-permute-start(bf16[192,2048]{1,0:T(8,128)(2,1)S(1)} %dynamic-slice_convert_fusion), channel_id=1, source_target_pairs={{0,1},{1,0},{2,3},{3,2},{4,5},{5,4},{6,7},{7,6},{8,9},{9,8},{10,11... | collective-permute-start | bytes 2359304 | tf_op jit(solution)/shard_map/ppermute | solution.py:74
Sparse Core Ops, SparseCore 0:
  9.8 37.4 all-gather.3
  49.1 33.2 all-gather.5
where the time goes:
time: 201 us
  waiting for transfers between devices  102 us (51%)
  starting transfers between devices  49.6 us (25%)
  matrix products  25.4 us (13%)
  between operations  14.3 us (7%)
  blocking collectives  5.47 us (3%)
  other arithmetic  3.09 us (2%)
    ppermute x12, starting transfers between devices, shifted(): return lax.ppermute(value, axis, pairs)  41.3 us
    ppermute x3, waiting for transfers between devices, summed(): arrived = lax.ppermute(other.astype(kind), 'dp', [(0, 1), (1, 0)])  26.9 us
    ppermute x12, waiting for transfers between devices, shifted(): return lax.ppermute(value, axis, pairs)  26.9 us
    all_gather x1, waiting for transfers between devices, on_device(): group_dy = lax.all_gather(cotangent, 'dp', axis=0, tiled=True)  26.1 us
    all_gather x1, waiting for transfers between devices, on_device(): group_x = lax.all_gather(tokens, 'dp', axis=0, tiled=True)  20.7 us
    ppermute x3, starting transfers between devices, summed(): arrived = lax.ppermute(other.astype(kind), 'dp', [(0, 1), (1, 0)])  8.21 us
    all_gather x1, blocking collectives, on_device(): group_gate = lax.all_gather(gate_probs, 'dp', axis=0, tiled=True)  5.47 us
  transfers between devices with their start and end apart: 17, of which 8 were waited for; matrix products, arithmetic and copies ran while one was open for 13% of the time, Pallas kernels for 0%

commit v1 on v0

--- a/solution.py
+++ b/solution.py
@@ -17,7 +17,9 @@
     half = lax.axis_index("dp")
     own = tokens.shape[0]
     group_x = lax.all_gather(tokens, "dp", axis=0, tiled=True)
-    group_dy = lax.all_gather(cotangent, "dp", axis=0, tiled=True)
+    group_dy = jnp.concatenate(
+        lax.all_to_all(jnp.stack([cotangent for _ in range(lax.axis_size("dp"))]), "dp", 0, 0), 0
+    )
     group_gate = lax.all_gather(gate_probs, "dp", axis=0, tiled=True)
     cycle, cap = slot_rows.shape
     group = group_x.shape[0]

time: 201 us -> 192 us (0.955)
  starting transfers between devices: 49.6 us -> 39.1 us
    all_gather x1 -> x0, waiting for transfers between devices: 26.1 us -> none  [on_device(): group_dy = lax.all_gather(cotangent, 'dp', axis=0, tiled=True)]
    ppermute x12, waiting for transfers between devices: 26.9 us -> 46.9 us  [shifted(): return lax.ppermute(value, axis, pairs)]
    ppermute x12, starting transfers between devices: 41.3 us -> 31.1 us  [shifted(): return lax.ppermute(value, axis, pairs)]
    all_gather x1, waiting for transfers between devices: 20.7 us -> 27.5 us  [on_device(): group_x = lax.all_gather(tokens, 'dp', axis=0, tiled=True)]
    ppermute x3, starting transfers between devices: 8.21 us -> 3.96 us  [summed(): arrived = lax.ppermute(other.astype(kind), 'dp', [(0, 1), (1, 0)])]
    all_to_all x0 -> x1, starting transfers between devices: none -> 4.02 us  [on_device(): lax.all_to_all(jnp.stack([cotangent for _ in range(lax.axis_size('dp'))])...]
  transfers between devices with their start and end apart: 17 -> 17, of which waited for: 8 -> 9; matrix products, arithmetic and copies ran while one was open for 13% -> 14% of each run, Pallas kernels for 0% -> 0%
where the time goes in v1:
time: 192 us
  waiting for transfers between devices  102 us (53%)
  starting transfers between devices  39.1 us (20%)
  matrix products  24.7 us (13%)
  between operations  14.3 us (7%)
  blocking collectives  5.67 us (3%)
  other arithmetic  4.37 us (2%)
  local copies, waits for them, and re-layouts  2.03 us (1%)
    ppermute x12, waiting for transfers between devices, shifted(): return lax.ppermute(value, axis, pairs)  46.9 us
    ppermute x12, starting transfers between devices, shifted(): return lax.ppermute(value, axis, pairs)  31.1 us
    all_gather x1, waiting for transfers between devices, on_device(): group_x = lax.all_gather(tokens, 'dp', axis=0, tiled=True)  27.5 us
    ppermute x3, waiting for transfers between devices, summed(): arrived = lax.ppermute(other.astype(kind), 'dp', [(0, 1), (1, 0)])  26.9 us
    all_gather x1, blocking collectives, on_device(): group_gate = lax.all_gather(gate_probs, 'dp', axis=0, tiled=True)  5.67 us
    all_to_all x1, starting transfers between devices, on_device(): lax.all_to_all(jnp.stack([cotangent for _ in range(lax.axis_size('dp'))])...  4.02 us
    ppermute x3, starting transfers between devices, summed(): arrived = lax.ppermute(other.astype(kind), 'dp', [(0, 1), (1, 0)])  3.96 us
  transfers between devices with their start and end apart: 17, of which 9 were waited for; matrix products, arithmetic and copies ran while one was open for 14% of the time, Pallas kernels for 0%

profile of v1, /device:TPU:1, one launch (start us, length us, event | category | flops | bytes accessed | tf_op | source)
XLA Modules:
  0.0 192.1 jit_solution(3043337603893390686)
XLA Ops:
  7.2 0.7 all-gather.3.cloned.1.call-update
  7.9 5.7 %all-gather = bf16[2,192,3]{1,2,0:T(4,128)(2,1)S(1)} all-gather(bf16[1,192,3]{1,2,0:T(4,128)(2,1)} %bitcast.80), channel_id=1, replica_groups=mesh['blk'=128,'dp'=2] {'dp'}, dimensions={0}, use_global_device_ids=true | all-gather | bytes 3456 | tf_op jit(solution)/shard_map/all_gather | solution.py:23
  13.7 1.0 fusion.27
  14.7 8.9 %collective-permute-start.3 = (bf16[128]{0:T(256)(128)(2,1)S(1)}, bf16[128]{0:T(256)(128)(2,1)S(1)}, u32[]{:S(2)}, u32[]{:S(2)}) collective-permute-start(bf16[128]{0:T(256)(128)(2,1)S(1)} %get-tuple-element.29), channel_id=1, source_target_pairs={{0,252},{2,254},{4,0},{6,2},{8,4},{10,6},{12,8},{14,10},{16,12},{1... | collective-permute-start | bytes 776 | tf_op jit(solution)/shard_map/ppermute | solution.py:13
  23.6 2.1 %collective-permute-start.2 = (bf16[128]{0:T(256)(128)(2,1)S(1)}, bf16[128]{0:T(256)(128)(2,1)S(1)}, u32[]{:S(2)}, u32[]{:S(2)}) collective-permute-start(bf16[128]{0:T(256)(128)(2,1)S(1)} %get-tuple-element.30), channel_id=1, source_target_pairs={{0,254},{2,0},{4,2},{6,4},{8,6},{10,8},{12,10},{14,12},{16,14},{18... | collective-permute-start | bytes 776 | tf_op jit(solution)/shard_map/ppermute | solution.py:13
  25.7 1.3 pad_maximum_fusion.1
  26.9 4.0 %all-to-all-start = ((bf16[2,192,2048]{2,1,0:T(8,128)(2,1)}), bf16[2,192,2048]{2,1,0:T(8,128)(2,1)S(1)}, u32[]{:S(2)}, u32[]{:S(2)}) async-start(bf16[2,192,2048]{2,1,0:T(8,128)(2,1)} %pad_maximum_fusion.1), calls=%async_computation | async-start | bytes 3145728 | tf_op jit(solution)/shard_map/all_to_all | solution.py:21
  31.0 0.1 iota_compare_fusion
  31.2 27.5 %all-gather.3.cloned.1.call-done = bf16[384,2048]{1,0:T(8,128)(2,1)} async-done(((bf16[192,2048]{1,0:T(8,128)(2,1)}), bf16[384,2048]{1,0:T(8,128)(2,1)}) %all-gather.3.cloned.1.call-update) | async-done | bytes 1572880 | tf_op jit(solution)/shard_map/all_gather | solution.py:19
  58.6 2.4 %convolution_convert_fusion.5 = bf16[3,128,2048]{2,1,0:T(8,128)(2,1)S(1)} fusion(bf16[384,2048]{1,0:T(8,128)(2,1)} %all-gather.3.cloned.1.call-done, s32[3,128]{1,0:T(4,128)S(1)} %copy-done.5), kind=kOutput, calls=%fused_computation.6 | convolution fusion | flops 604913664 | bytes 3147264 | tf_op jit(solution)/shard_map/sct,td->scd/dot_general | solution.py:28
  61.1 1.2 slice_bitcast_fusion.5
  62.3 10.7 %collective-permute-start.1 = (bf16[128,2048]{1,0:T(8,128)(2,1)}, bf16[128,2048]{1,0:T(8,128)(2,1)}, u32[]{:S(2)}, u32[]{:S(2)}) collective-permute-start(bf16[128,2048]{1,0:T(8,128)(2,1)} %get-tuple-element.21), channel_id=1, source_target_pairs={{0,252},{2,254},{4,0},{6,2},{8,4},{10,6},{12,8},{14,10},{16,12},{1... | collective-permute-start | bytes 1572872 | tf_op jit(solution)/shard_map/ppermute | solution.py:13
  73.0 1.0 collective-permute-start
  74.0 1.0 convolution_convert_fusion.3
  75.1 0.3 collective-permute-start.8
  75.5 0.3 collective-permute-start.7
  75.8 8.1 %collective-permute-done.1 = bf16[128,2048]{1,0:T(8,128)(2,1)} collective-permute-done((bf16[128,2048]{1,0:T(8,128)(2,1)}, bf16[128,2048]{1,0:T(8,128)(2,1)}, u32[]{:S(2)}, u32[]{:S(2)}) %collective-permute-start.1) | collective-permute-done | bytes 524320 | tf_op jit(solution)/shard_map/ppermute | solution.py:13
  83.8 5.4 %collective-permute-done = bf16[128,2048]{1,0:T(8,128)(2,1)} collective-permute-done((bf16[128,2048]{1,0:T(8,128)(2,1)}, bf16[128,2048]{1,0:T(8,128)(2,1)}, u32[]{:S(2)}, u32[]{:S(2)}) %collective-permute-start) | collective-permute-done | bytes 524320 | tf_op jit(solution)/shard_map/ppermute | solution.py:13
  89.2 2.3 %fusion.19 = f32[384,384]{0,1:T(8,128)S(1)} fusion(bf16[1,2048,384]{2,1,0:T(8,128)(2,1)S(1)} %copy-done.2, bf16[128,2048]{1,0:T(8,128)(2,1)} %collective-permute-done.1, bf16[128,2048]{1,0:T(8,128)(2,1)} %collective-permute-done, bf16[128,2048]{1,0:T(8,128)(2,1)S(1)} %copy-done.4), kind=kOutput, calls=%fused_computation.29 | convolution fusion | flops 608698368 | bytes 3735552 | tf_op jit(solution)/shard_map/dot_general | solution.py:41
  91.6 2.2 %fusion.23 = f32[384,384]{0,1:T(8,128)S(1)} fusion(bf16[1,2048,384]{2,1,0:T(8,128)(2,1)S(1)} %copy-done.1, bf16[128,2048]{1,0:T(8,128)(2,1)} %collective-permute-done.1, bf16[128,2048]{1,0:T(8,128)(2,1)} %collective-permute-done, bf16[128,2048]{1,0:T(8,128)(2,1)S(1)} %copy-done.4), kind=kOutput, calls=%fused_computation.33 | convolution fusion | flops 608698368 | bytes 3735552 | tf_op jit(solution)/shard_map/dot_general | solution.py:40
  93.9 1.1 collective-permute-done.8
  95.0 5.4 %collective-permute-done.7 = bf16[128,2048]{1,0:T(8,128)(2,1)S(1)} collective-permute-done((bf16[128,2048]{1,0:T(8,128)(2,1)S(1)}, bf16[128,2048]{1,0:T(8,128)(2,1)S(1)}, u32[]{:S(2)}, u32[]{:S(2)}) %collective-permute-start.7) | collective-permute-done | bytes 524320 | tf_op jit(solution)/shard_map/ppermute | solution.py:13
  100.4 1.2 multiply_reduce_fusion
  101.6 1.0 convolution_convert_fusion.4
  102.7 1.6 collective-permute-start.5
  104.3 0.1 collective-permute-start.4
  104.4 1.0 fusion.21
  105.4 1.0 add_convert_fusion
  106.5 0.2 fusion.37
  106.7 1.5 collective-permute-start.10
  108.2 3.3 %collective-permute-start.13 = (f32[128]{0:T(128)S(1)}, f32[128]{0:T(128)S(1)}, u32[]{:S(2)}, u32[]{:S(2)}) collective-permute-start(f32[128]{0:T(128)S(1)} %get-tuple-element.26), channel_id=1, source_target_pairs={{0,4},{2,6},{4,8},{6,10},{8,12},{10,14},{12,16},{14,18},{16,20},{1... | collective-permute-start | bytes 1544 | tf_op jit(solution)/shard_map/ppermute | solution.py:13
  111.5 1.2 collective-permute-start.12
  112.8 3.5 %fusion = bf16[1,2048,384]{2,1,0:T(8,128)(2,1)} fusion(bf16[384,384]{0,1:T(8,128)(2,1)S(1)} %get-tuple-element.10, bf16[128,2048]{1,0:T(8,128)(2,1)} %collective-permute-done.1, bf16[128,2048]{1,0:T(8,128)(2,1)} %collective-permute-done, bf16[128,2048]{1,0:T(8,128)(2,1)S(1)} %copy-done.4), kind=kOutput, calls=%fused_computation.7 | convolution fusion | flops 609484800 | bytes 3440640 | tf_op jit(solution)/shard_map/cd,ch->dh/dot_general | solution.py:61
  116.3 3.5 %fusion.1 = bf16[1,2048,384]{2,1,0:T(8,128)(2,1)} fusion(bf16[384,384]{0,1:T(8,128)(2,1)S(1)} %get-tuple-element.24, bf16[128,2048]{1,0:T(8,128)(2,1)} %collective-permute-done.1, bf16[128,2048]{1,0:T(8,128)(2,1)} %collective-permute-done, bf16[128,2048]{1,0:T(8,128)(2,1)S(1)} %copy-done.4), kind=kOutput, calls=%fused_computation.8 | convolution fusion | flops 609484800 | bytes 3440640 | tf_op jit(solution)/shard_map/cd,ch->dh/dot_general | solution.py:62
  119.8 25.4 %collective-permute-done.13 = f32[128]{0:T(128)S(1)} collective-permute-done((f32[128]{0:T(128)S(1)}, f32[128]{0:T(128)S(1)}, u32[]{:S(2)}, u32[]{:S(2)}) %collective-permute-start.13) | collective-permute-done | bytes 544 | tf_op jit(solution)/shard_map/ppermute | solution.py:13
  145.2 0.2 select_reduce_fusion.2
  145.5 0.8 collective-permute-start.14
  146.3 1.1 fusion.3
  147.5 2.3 %collective-permute-start.6 = (bf16[192,2048]{1,0:T(8,128)(2,1)S(1)}, bf16[192,2048]{1,0:T(8,128)(2,1)S(1)}, u32[]{:S(2)}, u32[]{:S(2)}) collective-permute-start(bf16[192,2048]{1,0:T(8,128)(2,1)S(1)} %dynamic-slice_convert_fusion.1), channel_id=1, source_target_pairs={{0,1},{1,0},{2,3},{3,2},{4,5},{5,4},{6,7},{7,6},{8,9},{9,8},{10,11... | collective-permute-start | bytes 2359304 | tf_op jit(solution)/shard_map/ppermute | solution.py:76
  149.8 1.5 collective-permute-done.9
  151.3 1.1 fusion.9
  152.5 0.9 collective-permute-start.11
  153.4 2.1 %fusion.2 = bf16[1,384,2048]{2,1,0:T(8,128)(2,1)} fusion(bf16[384,384]{0,1:T(8,128)(2,1)S(1)} %get-tuple-element.23, bf16[128,2048]{1,0:T(8,128)(2,1)S(1)} %collective-permute-done.8, bf16[128,2048]{1,0:T(8,128)(2,1)S(1)} %collective-permute-done.7, bf16[128,2048]{1,0:T(8,128)(2,1)S(1)} %get-tuple-element.14), kind=kOutput, calls=%fused_computation.9 | convolution fusion | flops 609484800 | bytes 3440640 | tf_op jit(solution)/shard_map/ch,cd->hd/dot_general | solution.py:63
  155.5 0.7 dynamic-slice_add_fusion
  156.2 11.1 %collective-permute-done.6 = bf16[192,2048]{1,0:T(8,128)(2,1)S(1)} collective-permute-done((bf16[192,2048]{1,0:T(8,128)(2,1)S(1)}, bf16[192,2048]{1,0:T(8,128)(2,1)S(1)}, u32[]{:S(2)}, u32[]{:S(2)}) %collective-permute-start.6) | collective-permute-done | bytes 786464 | tf_op jit(solution)/shard_map/ppermute | solution.py:76
  167.3 1.1 add_convert_fusion.2
  168.4 15.8 %collective-permute-done.11 = bf16[192,2048]{1,0:T(8,128)(2,1)S(1)} collective-permute-done((bf16[192,2048]{1,0:T(8,128)(2,1)S(1)}, bf16[192,2048]{1,0:T(8,128)(2,1)S(1)}, u32[]{:S(2)}, u32[]{:S(2)}) %collective-permute-start.11) | collective-permute-done | bytes 786464 | tf_op jit(solution)/shard_map/ppermute | solution.py:76
  184.2 1.1 add_convert_fusion.1
  (37 shorter events, 0.8 us)
Async XLA Ops:
  7.2 93.2 %copy-start = (bf16[1,384,2048]{2,1,0:T(8,128)(2,1)S(1)}, bf16[1,384,2048]{2,1,0:T(8,128)(2,1)}, u32[]{:S(2)}) copy-start(bf16[1,384,2048]{2,1,0:T(8,128)(2,1)} %param.13) | copy-start | bytes 4718596
  7.2 18.5 %copy-start.3 = (bf16[192,2048]{1,0:T(8,128)(2,1)S(1)}, bf16[192,2048]{1,0:T(8,128)(2,1)}, u32[]{:S(2)}) copy-start(bf16[192,2048]{1,0:T(8,128)(2,1)} %param.8) | copy-start | bytes 2359300
  7.2 51.4 %all-gather.3.cloned.1.call-start = ((), (), s32[]{:S(2)}) async-start(), calls=%async_computation.1 | async-start | bytes 2359296 | tf_op jit(solution)/shard_map/all_gather | solution.py:19
  14.7 16.4 %collective-permute-start.3 = (bf16[128]{0:T(256)(128)(2,1)S(1)}, bf16[128]{0:T(256)(128)(2,1)S(1)}, u32[]{:S(2)}, u32[]{:S(2)}) collective-permute-start(bf16[128]{0:T(256)(128)(2,1)S(1)} %get-tuple-element.29), channel_id=1, source_target_pairs={{0,252},{2,254},{4,0},{6,2},{8,4},{10,6},{12,8},{14,10},{16,12},{1... | collective-permute-start | bytes 776 | tf_op jit(solution)/shard_map/ppermute | solution.py:13
  23.6 7.6 %collective-permute-start.2 = (bf16[128]{0:T(256)(128)(2,1)S(1)}, bf16[128]{0:T(256)(128)(2,1)S(1)}, u32[]{:S(2)}, u32[]{:S(2)}) collective-permute-start(bf16[128]{0:T(256)(128)(2,1)S(1)} %get-tuple-element.30), channel_id=1, source_target_pairs={{0,254},{2,0},{4,2},{6,4},{8,6},{10,8},{12,10},{14,12},{16,14},{18... | collective-permute-start | bytes 776 | tf_op jit(solution)/shard_map/ppermute | solution.py:13
  26.9 4.0 %copy-start.5 = (s32[3,128]{1,0:T(4,128)S(1)}, s32[3,128]{1,0:T(4,128)}, u32[]{:S(2)}) copy-start(s32[3,128]{1,0:T(4,128)} %param.10) | copy-start | bytes 4612
  26.9 47.0 %all-to-all-start = ((bf16[2,192,2048]{2,1,0:T(8,128)(2,1)}), bf16[2,192,2048]{2,1,0:T(8,128)(2,1)S(1)}, u32[]{:S(2)}, u32[]{:S(2)}) async-start(bf16[2,192,2048]{2,1,0:T(8,128)(2,1)} %pad_maximum_fusion.1), calls=%async_computation | async-start | bytes 3145728 | tf_op jit(solution)/shard_map/all_to_all | solution.py:21
  62.3 21.6 %collective-permute-start.1 = (bf16[128,2048]{1,0:T(8,128)(2,1)}, bf16[128,2048]{1,0:T(8,128)(2,1)}, u32[]{:S(2)}, u32[]{:S(2)}) collective-permute-start(bf16[128,2048]{1,0:T(8,128)(2,1)} %get-tuple-element.21), channel_id=1, source_target_pairs={{0,252},{2,254},{4,0},{6,2},{8,4},{10,6},{12,8},{14,10},{16,12},{1... | collective-permute-start | bytes 1572872 | tf_op jit(solution)/shard_map/ppermute | solution.py:13
  73.0 16.3 %collective-permute-start = (bf16[128,2048]{1,0:T(8,128)(2,1)}, bf16[128,2048]{1,0:T(8,128)(2,1)}, u32[]{:S(2)}, u32[]{:S(2)}) collective-permute-start(bf16[128,2048]{1,0:T(8,128)(2,1)} %get-tuple-element.22), channel_id=1, source_target_pairs={{0,254},{2,0},{4,2},{6,4},{8,6},{10,8},{12,10},{14,12},{16,14},{18... | collective-permute-start | bytes 1572872 | tf_op jit(solution)/shard_map/ppermute | solution.py:13
  75.0 14.2 %copy-start.2 = (bf16[1,2048,384]{2,1,0:T(8,128)(2,1)S(1)}, bf16[1,2048,384]{2,1,0:T(8,128)(2,1)}, u32[]{:S(2)}) copy-start(bf16[1,2048,384]{2,1,0:T(8,128)(2,1)} %param.12) | copy-start | bytes 4718596
  75.0 14.2 %copy-start.4 = (bf16[128,2048]{1,0:T(8,128)(2,1)S(1)}, bf16[128,2048]{1,0:T(8,128)(2,1)}, u32[]{:S(2)}) copy-start(bf16[128,2048]{1,0:T(8,128)(2,1)} %get-tuple-element.20) | copy-start | bytes 1572868
  75.1 19.8 %collective-permute-start.8 = (bf16[128,2048]{1,0:T(8,128)(2,1)S(1)}, bf16[128,2048]{1,0:T(8,128)(2,1)S(1)}, u32[]{:S(2)}, u32[]{:S(2)}) collective-permute-start(bf16[128,2048]{1,0:T(8,128)(2,1)S(1)} %get-tuple-element.15), channel_id=1, source_target_pairs={{0,252},{2,254},{4,0},{6,2},{8,4},{10,6},{12,8},{14,10},{16,12},{1... | collective-permute-start | bytes 1572872 | tf_op jit(solution)/shard_map/ppermute | solution.py:13
  75.5 24.9 %collective-permute-start.7 = (bf16[128,2048]{1,0:T(8,128)(2,1)S(1)}, bf16[128,2048]{1,0:T(8,128)(2,1)S(1)}, u32[]{:S(2)}, u32[]{:S(2)}) collective-permute-start(bf16[128,2048]{1,0:T(8,128)(2,1)S(1)} %get-tuple-element.16), channel_id=1, source_target_pairs={{0,254},{2,0},{4,2},{6,4},{8,6},{10,8},{12,10},{14,12},{16,14},{18... | collective-permute-start | bytes 1572872 | tf_op jit(solution)/shard_map/ppermute | solution.py:13
  89.2 2.4 %copy-start.1 = (bf16[1,2048,384]{2,1,0:T(8,128)(2,1)S(1)}, bf16[1,2048,384]{2,1,0:T(8,128)(2,1)}, u32[]{:S(2)}) copy-start(bf16[1,2048,384]{2,1,0:T(8,128)(2,1)} %param.11) | copy-start | bytes 4718596
  102.7 43.6 %collective-permute-start.5 = (bf16[128,2048]{1,0:T(8,128)(2,1)S(1)}, bf16[128,2048]{1,0:T(8,128)(2,1)S(1)}, u32[]{:S(2)}, u32[]{:S(2)}) collective-permute-start(bf16[128,2048]{1,0:T(8,128)(2,1)S(1)} %get-tuple-element.18), channel_id=1, source_target_pairs={{0,4},{2,6},{4,8},{6,10},{8,12},{10,14},{12,16},{14,18},{16,20},{1... | collective-permute-start | bytes 1572872 | tf_op jit(solution)/shard_map/ppermute | solution.py:13
  104.3 42.0 %collective-permute-start.4 = (bf16[128,2048]{1,0:T(8,128)(2,1)S(1)}, bf16[128,2048]{1,0:T(8,128)(2,1)S(1)}, u32[]{:S(2)}, u32[]{:S(2)}) collective-permute-start(bf16[128,2048]{1,0:T(8,128)(2,1)S(1)} %get-tuple-element.19), channel_id=1, source_target_pairs={{0,2},{2,4},{4,6},{6,8},{8,10},{10,12},{12,14},{14,16},{16,18},{18... | collective-permute-start | bytes 1572872 | tf_op jit(solution)/shard_map/ppermute | solution.py:13
  106.7 43.1 %collective-permute-start.10 = (bf16[128,2048]{1,0:T(8,128)(2,1)S(1)}, bf16[128,2048]{1,0:T(8,128)(2,1)S(1)}, u32[]{:S(2)}, u32[]{:S(2)}) collective-permute-start(bf16[128,2048]{1,0:T(8,128)(2,1)S(1)} %get-tuple-element.12), channel_id=1, source_target_pairs={{0,4},{2,6},{4,8},{6,10},{8,12},{10,14},{12,16},{14,18},{16,20},{1... | collective-permute-start | bytes 1572872 | tf_op jit(solution)/shard_map/ppermute | solution.py:13
  108.2 37.0 %collective-permute-start.13 = (f32[128]{0:T(128)S(1)}, f32[128]{0:T(128)S(1)}, u32[]{:S(2)}, u32[]{:S(2)}) collective-permute-start(f32[128]{0:T(128)S(1)} %get-tuple-element.26), channel_id=1, source_target_pairs={{0,4},{2,6},{4,8},{6,10},{8,12},{10,14},{12,16},{14,18},{16,20},{1... | collective-permute-start | bytes 1544 | tf_op jit(solution)/shard_map/ppermute | solution.py:13
  111.5 33.6 %collective-permute-start.12 = (f32[128]{0:T(128)S(1)}, f32[128]{0:T(128)S(1)}, u32[]{:S(2)}, u32[]{:S(2)}) collective-permute-start(f32[128]{0:T(128)S(1)} %get-tuple-element.25), channel_id=1, source_target_pairs={{0,2},{2,4},{4,6},{6,8},{8,10},{10,12},{12,14},{14,16},{16,18},{18... | collective-permute-start | bytes 1544 | tf_op jit(solution)/shard_map/ppermute | solution.py:13
  145.2 6.1 %collective-permute-start.9 = (bf16[128,2048]{1,0:T(8,128)(2,1)S(1)}, bf16[128,2048]{1,0:T(8,128)(2,1)S(1)}, u32[]{:S(2)}, u32[]{:S(2)}) collective-permute-start(bf16[128,2048]{1,0:T(8,128)(2,1)S(1)} %get-tuple-element.13), channel_id=1, source_target_pairs={{0,2},{2,4},{4,6},{6,8},{8,10},{10,12},{12,14},{14,16},{16,18},{18... | collective-permute-start | bytes 1572872 | tf_op jit(solution)/shard_map/ppermute | solution.py:13
  145.5 10.1 %collective-permute-start.14 = (f32[192,3]{0,1:T(4,128)S(1)}, f32[192,3]{0,1:T(4,128)S(1)}, u32[]{:S(2)}, u32[]{:S(2)}) collective-permute-start(f32[192,3]{0,1:T(4,128)S(1)} %constant_dynamic-slice_fusion), channel_id=1, source_target_pairs={{0,1},{1,0},{2,3},{3,2},{4,5},{5,4},{6,7},{7,6},{8,9},{9,8},{10,11... | collective-permute-start | bytes 6920 | tf_op jit(solution)/shard_map/ppermute | solution.py:76
  147.5 19.8 %collective-permute-start.6 = (bf16[192,2048]{1,0:T(8,128)(2,1)S(1)}, bf16[192,2048]{1,0:T(8,128)(2,1)S(1)}, u32[]{:S(2)}, u32[]{:S(2)}) collective-permute-start(bf16[192,2048]{1,0:T(8,128)(2,1)S(1)} %dynamic-slice_convert_fusion.1), channel_id=1, source_target_pairs={{0,1},{1,0},{2,3},{3,2},{4,5},{5,4},{6,7},{7,6},{8,9},{9,8},{10,11... | collective-permute-start | bytes 2359304 | tf_op jit(solution)/shard_map/ppermute | solution.py:76
  152.5 31.7 %collective-permute-start.11 = (bf16[192,2048]{1,0:T(8,128)(2,1)S(1)}, bf16[192,2048]{1,0:T(8,128)(2,1)S(1)}, u32[]{:S(2)}, u32[]{:S(2)}) collective-permute-start(bf16[192,2048]{1,0:T(8,128)(2,1)S(1)} %dynamic-slice_convert_fusion), channel_id=1, source_target_pairs={{0,1},{1,0},{2,3},{3,2},{4,5},{5,4},{6,7},{7,6},{8,9},{9,8},{10,11... | collective-permute-start | bytes 2359304 | tf_op jit(solution)/shard_map/ppermute | solution.py:76
Sparse Core Ops, SparseCore 0:
  9.8 48.7 all-gather.2
